TPU v7x, 32 devices: a whole 2x2x4 slice. The times are simulated.
32 devices in a mesh: beam: 2 (over y), inp: 8 (over z, x), span: 2 (over core).
Axes of the slice: x: 2, y: 2, z: 4, core: 2. Of those that a mesh axis runs over, the one named last changes fastest.
Arguments:
- voltages: bfloat16 [2, 8, 1024, 16384], P(None, 'beam', 'inp', 'span'), parts along dimension 1, may hold values from -6 to 6
- gains: float32 [2, 8, 1024, 32], P(None, 'beam', 'inp'), parts along dimension 1, may hold values from -4 to 4
Outputs:
- visibilities: bfloat16 [256, 1024, 1024], P(('beam', 'inp'), 'span'), parts along dimension 0
There are 2 independent parts, one for each index of `beam`. A program takes and returns all parts, laid end to end along the dimension named above; each array names one. Nothing has to cross between parts.
All inputs are finite; a program needn't handle non-finite values.
Results may differ from a plain program's by a relative error of at most 0.0085.
Values may be sent and summed in bfloat16 or wider, within the bound.
A program may use at most 192 MiB of HBM per device.

v0:
```python
import math

import jax
import jax.numpy as jnp
from jax import lax
from jax.sharding import PartitionSpec as P

FINE = 32
TAPS = 4


def prototype(tap_count, fine_count):
    length = tap_count * fine_count
    offsets = jnp.arange(length).astype(jnp.float32)
    shifted = (offsets - length / 2 + 0.5) / fine_count
    taper = 0.5 - 0.5 * jnp.cos(2.0 * math.pi * (offsets + 0.5) / length)
    window = jnp.sinc(shifted) * taper
    window = window / jnp.sqrt(jnp.sum(window * window))
    return window.reshape(tap_count, fine_count)


def kernels(window, fine_count):
    points = jnp.arange(fine_count)
    phase_steps = points[:, None] * points[None, :] % fine_count
    angles = 2.0 * math.pi * phase_steps.astype(jnp.float32) / fine_count
    cosine = jnp.cos(angles)
    sine_part = jnp.sin(angles)
    result = []
    for tap_index in range(window.shape[0]):
        weights = window[tap_index][:, None]
        hcos = weights * cosine
        hsin = weights * sine_part
        result.append(jnp.stack([jnp.stack([hcos, -hsin]), jnp.stack([hsin, hcos])]))
    return jnp.stack(result)


def packed_rows(left_rows, right_rows, left_all, row_start):
    real_sums = jnp.einsum("cif,cjf->cij", left_rows, left_all, preferred_element_type=jnp.float32)
    imag_sums = jnp.einsum("cif,cjf->cij", right_rows, left_all, preferred_element_type=jnp.float32)
    row_index = row_start + jnp.arange(left_rows.shape[1])
    col_index = jnp.arange(left_all.shape[1])
    upper = row_index[:, None] <= col_index[None, :]
    return jnp.where(upper[None], real_sums, imag_sums)


def local(voltages, gains):
    coarse = voltages.shape[1]
    local_inputs = voltages.shape[2]
    samples = voltages.shape[3]
    frames = samples // FINE
    window = prototype(TAPS, FINE)
    filters = kernels(window, FINE)
    filter_table = jnp.transpose(filters, (1, 0, 3, 2, 4))
    filter_high = filter_table.astype(jnp.bfloat16)
    filter_low = (filter_table - filter_high.astype(jnp.float32)).astype(jnp.bfloat16)
    padded = jnp.pad(voltages, ((0, 0), (0, 0), (0, 0), (0, (TAPS - 1) * FINE)))
    stacked = jnp.stack(
        [padded[..., tap_index * FINE : tap_index * FINE + samples] for tap_index in range(TAPS)],
        axis=1,
    )
    stacked = stacked.reshape(2, TAPS, coarse, local_inputs, frames, FINE)
    spectra = jnp.einsum(
        "atcnmp,atpbk->bcknm", stacked, filter_high, preferred_element_type=jnp.float32
    )
    spectra = spectra + jnp.einsum(
        "atcnmp,atpbk->bcknm", stacked, filter_low, preferred_element_type=jnp.float32
    )
    gain_real = jnp.swapaxes(gains[0], 1, 2)[:, :, :, None]
    gain_imag = jnp.swapaxes(gains[1], 1, 2)[:, :, :, None]
    real_part = spectra[0] * gain_real - spectra[1] * gain_imag
    imag_part = spectra[0] * gain_imag + spectra[1] * gain_real
    outgoing = jnp.stack([real_part, imag_part]).astype(jnp.bfloat16)
    outgoing = outgoing.reshape(2, coarse * FINE, local_inputs, frames)
    turned = lax.all_to_all(outgoing, "inp", split_axis=1, concat_axis=2, tiled=True)
    inputs = turned.shape[2]
    span_count = lax.axis_size("span")
    row_count = inputs // span_count
    frame_scale = 1.0 / (span_count * frames)
    row_start = lax.axis_index("span") * row_count
    frame_piece = lax.all_gather(turned, "span", axis=3, tiled=True)
    left_all = jnp.concatenate([frame_piece[0], frame_piece[1]], axis=-1)
    own_rows = lax.dynamic_slice_in_dim(frame_piece, row_start, row_count, 2)
    left_rows = jnp.concatenate([own_rows[0], own_rows[1]], axis=-1)
    right_rows = jnp.concatenate([own_rows[1], -own_rows[0]], axis=-1)
    summed = packed_rows(left_rows, right_rows, left_all, row_start) * frame_scale
    return summed.astype(jnp.bfloat16)


def solution(mesh):
    placed = (P(None, "beam", "inp", "span"), P(None, "beam", "inp", None))
    return jax.shard_map(
        local,
        mesh=mesh,
        in_specs=placed,
        out_specs=P(("beam", "inp"), "span", None),
        check_vma=False,
    )
```

profile of v0, /device:TPU:13, one launch (start us, length us, event | category | flops | bytes accessed | tf_op | source)
XLA Modules:
  0.0 863.4 jit_solution(2377499240589222631)
XLA Ops:
  6.5 0.7 multiply_reduce_fusion
  8.0 21.2 %copy.28 = bf16[2,4,128,8192]{2,3,1,0:T(8,128)(2,1)} copy(bf16[2,4,128,8192]{3,2,1,0:T(8,128)(2,1)} %param.2) | data formatting | bytes 33554432 | tf_op args[0]
  29.2 32.5 %pad_slice_fusion.2 = (bf16[2,4,128,8192]{2,3,1,0:T(8,128)(2,1)}, bf16[2,4,128,8192]{2,3,1,0:T(8,128)(2,1)}, bf16[2,4,128,8192]{2,3,1,0:T(8,128)(2,1)}) fusion(bf16[2,4,128,8192]{2,3,1,0:T(8,128)(2,1)} %copy.28), kind=kLoop, calls=%fused_computation.22 | loop fusion | bytes 67108864 | tf_op jit(solution)/shard_map/slice | solution.py:58
  61.6 30.6 %copy.31 = bf16[2,1,4,128,256,32]{4,5,1,0,3,2:T(8,128)(2,1)} copy(bf16[2,1,4,128,256,32]{3,5,4,2,0,1:T(8,128)(2,1)} %bitcast.137) | data formatting | bytes 33554432 | tf_op jit(solution)/shard_map/stack | solution.py:57
  92.3 30.7 %copy.32 = bf16[2,1,4,128,256,32]{4,5,1,0,3,2:T(8,128)(2,1)} copy(bf16[2,1,4,128,256,32]{3,5,4,2,0,1:T(8,128)(2,1)} %bitcast.136) | data formatting | bytes 33554432 | tf_op jit(solution)/shard_map/stack | solution.py:57
  122.9 30.7 %copy.33 = bf16[2,1,4,128,256,32]{4,5,1,0,3,2:T(8,128)(2,1)} copy(bf16[2,1,4,128,256,32]{3,5,4,2,0,1:T(8,128)(2,1)} %bitcast.135) | data formatting | bytes 33554432 | tf_op jit(solution)/shard_map/stack | solution.py:57
  153.6 30.7 %copy.30 = bf16[2,1,4,128,256,32]{4,5,1,0,3,2:T(8,128)(2,1)} copy(bf16[2,1,4,128,256,32]{3,5,4,2,0,1:T(8,128)(2,1)} %bitcast.132) | data formatting | bytes 33554432 | tf_op jit(solution)/shard_map/stack | solution.py:57
  184.6 36.7 %fusion.1 = f32[2,32,4,128,256,1,1]{4,1,6,5,3,2,0:T(8,128)} fusion(bf16[2,1,4,128,256,32]{4,5,1,0,3,2:T(8,128)(2,1)} %copy.33, bf16[2,1,4,128,256,32]{4,5,1,0,3,2:T(8,128)(2,1)} %copy.32, bf16[2,1,4,128,256,32]{4,5,1,0,3,2:T(8,128)(2,1)} %copy.31, bf16[2,1,4,128,256,32]{4,5,1,0,3,2:T(8,128)(2,1)} %copy.30, ...), kind=kOutput, calls=%fused_computation.5 | convolution fusion | flops 4563521536 | bytes 100728832 | tf_op jit(solution)/shard_map/atcnmp,atpbk->bcknm/dot_general | solution.py:65
  221.2 44.4 %fusion = f32[2,4,32,128,256]{4,2,3,1,0:T(8,128)} fusion(f32[2,32,4,128,256,1,1]{4,1,6,5,3,2,0:T(8,128)} %fusion.1, bf16[2,1,4,128,256,32]{4,5,1,0,3,2:T(8,128)(2,1)} %copy.33, bf16[2,1,4,128,256,32]{4,5,1,0,3,2:T(8,128)(2,1)} %copy.32, bf16[2,1,4,128,256,32]{4,5,1,0,3,2:T(8,128)(2,1)} %copy.31, bf16[2,1,4,128,256,32]{4,5,1,0,3,2:T(8,128)(2,1)} %copy.30, ...), kind=kOutput, calls=%fused_computation.3 | convolution fusion | flops 4571926528 | bytes 134283264 | tf_op jit(solution)/shard_map/atcnmp,atpbk->bcknm/dot_general | solution.py:62
  265.7 0.1 copy.34
  265.9 17.8 %subtract_convert_fusion = (bf16[1,4,32,128,256]{4,2,3,1,0:T(8,128)(2,1)}, bf16[1,4,32,128,256]{4,2,3,1,0:T(8,128)(2,1)}) fusion(f32[2,4,32,128,256]{4,2,3,1,0:T(8,128)} %fusion, f32[4,32,128]{1,2,0:T(8,128)S(1)} %copy.35, f32[4,32,128]{1,2,0:T(8,128)S(1)} %copy.34), kind=kLoop, calls=%fused_computation.19 | loop fusion | flops 33554432 | bytes 50462720 | tf_op jit(solution)/shard_map/convert.3
  283.8 11.5 %copy.36 = bf16[1,4,32,128,256]{4,3,2,1,0:T(8,128)(2,1)} copy(bf16[1,4,32,128,256]{4,2,3,1,0:T(8,128)(2,1)} %get-tuple-element.7) | data formatting | bytes 16777216 | tf_op jit(solution)/shard_map/convert.3
  295.2 11.6 %copy.37 = bf16[1,4,32,128,256]{4,3,2,1,0:T(8,128)(2,1)} copy(bf16[1,4,32,128,256]{4,2,3,1,0:T(8,128)(2,1)} %get-tuple-element.8) | data formatting | bytes 16777216 | tf_op jit(solution)/shard_map/convert.2
  306.9 8.0 pad_maximum_fusion.3
  314.9 2.0 copy.38
  316.9 366.5 %all_to_all.18 = bf16[2,128,128,256]{3,2,0,1:T(8,128)(2,1)S(1)} all-to-all(bf16[2,128,128,256]{3,2,0,1:T(8,128)(2,1)S(1)} %copy.38), channel_id=1, replica_groups=mesh['beam'=2,'inp'=8,'span'=2] {'inp'}, dimensions={1} | all-to-all | bytes 33554432 | tf_op jit(solution)/shard_map/all_to_all | solution.py:74
  683.3 6.5 copy.40
  689.9 0.4 iota_compare_fusion
  690.3 52.3 %all-gather.2.cloned.1.call-done = bf16[2,16,1024,512]{3,2,1,0:T(8,128)(2,1)} async-done(((bf16[2,16,1024,256]{3,2,1,0:T(8,128)(2,1)}), bf16[2,16,1024,512]{3,2,1,0:T(8,128)(2,1)}) %all-gather.2.cloned.1.call-update) | async-done | bytes 33554448 | tf_op jit(solution)/shard_map/all_gather | solution.py:80
  742.6 22.5 %slice_bitcast_fusion.1 = (bf16[16,1024,512]{2,1,0:T(8,128)(2,1)}, bf16[16,1024,512]{2,1,0:T(8,128)(2,1)}) fusion(bf16[2,16,1024,512]{3,2,1,0:T(8,128)(2,1)} %all-gather.2.cloned.1.call-done), kind=kLoop, calls=%fused_computation.10 | loop fusion | bytes 67108864 | tf_op jit(solution)/shard_map/squeeze | solution.py:81
  765.0 10.3 %fusion.44 = (bf16[16,512,512]{2,1,0:T(8,128)(2,1)}, bf16[16,512,512]{2,1,0:T(8,128)(2,1)}) fusion(bf16[2,16,1024,512]{3,2,1,0:T(8,128)(2,1)} %all-gather.2.cloned.1.call-done, s32[]{:T(128)S(6)} %select_n.117), kind=kLoop, calls=%fused_computation.91 | loop fusion | flops 12582912 | bytes 25165828 | tf_op jit(solution)/shard_map/neg | solution.py:84
  775.3 7.4 dynamic-slice_bitcast_fusion
  782.7 36.8 %fusion.3 = f32[16,512,1024]{2,1,0:T(8,128)} fusion(bf16[16,1024,512]{2,1,0:T(8,128)(2,1)} %get-tuple-element.10, bf16[16,1024,512]{2,1,0:T(8,128)(2,1)} %get-tuple-element.9, bf16[16,512,512]{2,1,0:T(8,128)(2,1)} %get-tuple-element.5, bf16[16,512,512]{2,1,0:T(8,128)(2,1)} %dynamic-slice_bitcast_fusion), kind=kOutput, calls=%fused_computation.7 | convolution fusion | flops 17280532480 | bytes 83886080 | tf_op jit(solution)/shard_map/cif,cjf->cij/dot_general | solution.py:39
  819.6 37.0 %multiply_convert_fusion = bf16[16,512,1024]{2,1,0:T(8,128)(2,1)} fusion(f32[16,512,1024]{2,1,0:T(8,128)} %fusion.3, pred[512,1024]{1,0:T(8,128)(4,1)S(1)} %iota_compare_fusion, bf16[16,1024,512]{2,1,0:T(8,128)(2,1)} %get-tuple-element.10, bf16[16,1024,512]{2,1,0:T(8,128)(2,1)} %get-tuple-element.9, bf16[16,512,512]{2,1,0:T(8,128)(2,1)} %dynamic-slice_bitcast_fusion, ...), kind=kOutput, calls=%fused_computation.4 | convolution fusion | flops 17305698304 | bytes 101187584 | tf_op jit(solution)/shard_map/cif,cjf->cij/dot_general | solution.py:38
  (18 shorter events, 0.5 us)
Async XLA Ops:
  6.5 736.0 %all-gather.2.cloned.1.call-start = ((), (), s32[]{:S(2)}) async-start(), calls=%async_computation.1 | async-start | bytes 50331648 | tf_op jit(solution)/shard_map/all_gather | solution.py:80
  221.2 44.4 %copy-start = (f32[2,4,128,32]{2,3,1,0:T(8,128)S(1)}, f32[2,4,128,32]{2,3,1,0:T(8,128)}, u32[]{:S(2)}) copy-start(f32[2,4,128,32]{2,3,1,0:T(8,128)} %param.3) | copy-start | bytes 393220
Sparse Core Ops, SparseCore 0:
  690.0 52.5 all-gather.1
where the time goes:
time: 868 us; the launch traced here: 863 us
  blocking collectives  366 us (42%)
  local copies, waits for them, and re-layouts  238 us (27%)
  matrix products  155 us (18%)
  waiting for transfers between devices  52.3 us (6%)
  other arithmetic  37.4 us (4%)
  between operations  14.2 us (2%)
    all_to_all x1, blocking collectives, local(): lax.all_to_all(outgoing, 'inp', split_axis=1, concat_axis=2, tiled=True)  366 us
    another operation x4, local copies, waits for them, and re-layouts, local(): jnp.stack([padded[..., tap_index * FINE:tap_index * FINE + samples] for t...  123 us
    all_gather x1, waiting for transfers between devices, local(): frame_piece = lax.all_gather(turned, 'span', axis=3, tiled=True)  52.3 us
    dot_general x1, matrix products, local(): jnp.einsum('atcnmp,atpbk->bcknm', stacked, filter_high, preferred_element...  44.4 us
    dot_general x1, matrix products, packed_rows(): jnp.einsum('cif,cjf->cij', left_rows, left_all, preferred_element_type=jn...  37 us
    dot_general x1, matrix products, packed_rows(): jnp.einsum('cif,cjf->cij', right_rows, left_all, preferred_element_type=j...  36.8 us
    dot_general x1, matrix products, local(): jnp.einsum('atcnmp,atpbk->bcknm', stacked, filter_low, preferred_element_...  36.7 us
    slice x1, local copies, waits for them, and re-layouts, local(): padded[..., tap_index * FINE:tap_index * FINE + samples]  32.5 us
  transfers between devices with their start and end apart: 1, of which 1 were waited for; matrix products, arithmetic and copies ran while one was open for 0% of the time, Pallas kernels for 0%

commit v1 on v0

--- a/solution.py
+++ b/solution.py
@@ -1,12 +1,17 @@
+import functools
 import math
 
 import jax
 import jax.numpy as jnp
+import numpy as np
 from jax import lax
+from jax.experimental import pallas as pl
+from jax.experimental.pallas import tpu as pltpu
 from jax.sharding import PartitionSpec as P
 
 FINE = 32
 TAPS = 4
+MESH = pl.DeviceIdType.MESH
 
 
 def prototype(tap_count, fine_count):
@@ -86,10 +91,332 @@
     return summed.astype(jnp.bfloat16)
 
 
+def order_of(step, mine, coarse):
+    if coarse == 4:
+        high = (mine // 2 + 1 - step // 2) % 2
+        low = (mine % 2 + (step + 1) // 2) % 2
+        return 2 * high + low
+    return (mine + step + 1) % coarse
+
+
+def filter_rows(fine_count, tap_count, group):
+    length = tap_count * fine_count
+    offsets = np.arange(length, dtype=np.float64)
+    shifted = (offsets - length / 2 + 0.5) / fine_count
+    taper = 0.5 - 0.5 * np.cos(2.0 * np.pi * (offsets + 0.5) / length)
+    window = np.sinc(shifted) * taper
+    window = window / np.sqrt(np.sum(window * window))
+    fine = np.arange(fine_count)
+    angles = 2.0 * np.pi * ((offsets[None, :] * fine[:, None]) % fine_count) / fine_count
+    hcos = window[None, :] * np.cos(angles)
+    hsin = window[None, :] * np.sin(angles)
+    span = group * fine_count + length
+    rows = np.zeros((group, 2, fine_count, 2, span), np.float64)
+    for frame in range(group):
+        at = slice(frame * fine_count, frame * fine_count + length)
+        rows[frame, 0, :, 0, at] = hcos
+        rows[frame, 0, :, 1, at] = hsin
+        rows[frame, 1, :, 0, at] = -hsin
+        rows[frame, 1, :, 1, at] = hcos
+    rows = rows.reshape(group * 2 * fine_count, 2 * span).astype(np.float32)
+    high = rows.astype(jnp.bfloat16)
+    low = (rows - high.astype(np.float32)).astype(jnp.bfloat16)
+    return high, low
+
+
+def fused_kernel(
+    dims, volt, gains, high, low, vis, send, recv,
+    xbuf, tbuf, stage, bbuf, lefts, rights, obuf,
+    xsem, stsem, ssem, rsem, psend, precv, bsem, osem,
+):
+    ranks, coarse, chunks, each, local_inputs, frames, scale = dims
+    halves = ranks // coarse
+    samples = frames * FINE
+    rows = ranks * local_inputs // 2
+    ahead = min(4, chunks)
+    early = min(2, chunks)
+    beam = lax.axis_index("beam")
+    me = lax.axis_index("inp")
+    span = lax.axis_index("span")
+    mine = me // halves
+    my_half = me % halves
+
+    def peer(step, turn):
+        return order_of(step, mine, coarse) * halves + (my_half + turn) % halves
+
+    peers = [(step, turn) for step in range(coarse) for turn in range(halves)]
+    peers = [pair for pair in peers if pair != (coarse - 1, 0)]
+
+    barrier = pltpu.get_barrier_semaphore()
+    for step, turn in peers:
+        pl.semaphore_signal(barrier, inc=1, device_id=(beam, peer(step, turn), span), device_id_type=MESH)
+    pl.semaphore_signal(barrier, inc=1, device_id=(beam, me, 1 - span), device_id_type=MESH)
+    pl.semaphore_wait(barrier, len(peers) + 1)
+
+    def load(step, slot):
+        block = order_of(step, mine, coarse)
+        return pltpu.make_async_copy(
+            volt.at[:, block], xbuf.at[slot, :, :, pl.ds(0, samples)], xsem.at[slot]
+        )
+
+    def outgoing(step, turn, chunk):
+        other = peer(step, turn)
+        return pltpu.make_async_remote_copy(
+            src_ref=send.at[other, chunk],
+            dst_ref=recv.at[span, chunk, me],
+            send_sem=ssem.at[chunk, other],
+            recv_sem=rsem.at[chunk, me],
+            device_id=(beam, other, span),
+            device_id_type=MESH,
+        )
+
+    def incoming(step, turn, chunk):
+        other = peer(step, turn)
+        return pltpu.make_async_remote_copy(
+            src_ref=send.at[other, chunk],
+            dst_ref=recv.at[span, chunk, other],
+            send_sem=ssem.at[chunk, other],
+            recv_sem=rsem.at[chunk, other],
+            device_id=(beam, other, span),
+            device_id_type=MESH,
+        )
+
+    def forward(chunk):
+        return pltpu.make_async_remote_copy(
+            src_ref=recv.at[span, chunk],
+            dst_ref=recv.at[span, chunk],
+            send_sem=psend.at[chunk],
+            recv_sem=precv.at[chunk],
+            device_id=(beam, me, 1 - span),
+            device_id_type=MESH,
+        )
+
+    def backward(chunk):
+        return pltpu.make_async_remote_copy(
+            src_ref=recv.at[1 - span, chunk],
+            dst_ref=recv.at[1 - span, chunk],
+            send_sem=psend.at[chunk],
+            recv_sem=precv.at[chunk],
+            device_id=(beam, me, 1 - span),
+            device_id_type=MESH,
+        )
+
+    tail = jnp.zeros((2, local_inputs, TAPS * FINE), jnp.bfloat16)
+    xbuf[0, :, :, pl.ds(samples, TAPS * FINE)] = tail
+    xbuf[1, :, :, pl.ds(samples, TAPS * FINE)] = tail
+
+    def channelize(step, slot):
+        block = order_of(step, mine, coarse)
+        load(step, slot).wait()
+
+        @pl.loop(0, frames // 8)
+        def _(pair):
+            base = pl.multiple_of(pair * (8 * FINE), 4 * FINE)
+            pieces = []
+            for part in range(2):
+                at = base + part * 4 * FINE
+                at = pl.multiple_of(at, 4 * FINE)
+                pieces.append(
+                    jnp.concatenate(
+                        [xbuf[slot, 0, :, pl.ds(at, 8 * FINE)], xbuf[slot, 1, :, pl.ds(at, 8 * FINE)]],
+                        axis=1,
+                    )
+                )
+            both = jnp.concatenate(pieces, axis=0)
+            contract = (((1,), (1,)), ((), ()))
+            got = lax.dot_general(high[...], both, contract, preferred_element_type=jnp.float32)
+            got = got + lax.dot_general(low[...], both, contract, preferred_element_type=jnp.float32)
+            at = pl.multiple_of(pair * (16 * FINE), 16 * FINE)
+            tbuf[pl.ds(at, 8 * FINE), :] = got[:, :local_inputs]
+            tbuf[pl.ds(at + 8 * FINE, 8 * FINE), :] = got[:, local_inputs:]
+
+        @pl.loop(0, FINE)
+        def _(fine):
+            half = fine // (chunks * each)
+            chunk = (fine // each) % chunks
+            index = fine % each
+            real = tbuf[pl.ds(fine, frames, stride=2 * FINE), :]
+            imag = tbuf[pl.ds(FINE + fine, frames, stride=2 * FINE), :]
+            gain_real = gains[block, 0, pl.ds(fine, 1), :]
+            gain_imag = gains[block, 1, pl.ds(fine, 1), :]
+            stage[half, chunk, index, 0] = (real * gain_real - imag * gain_imag).astype(jnp.bfloat16)
+            stage[half, chunk, index, 1] = (real * gain_imag + imag * gain_real).astype(jnp.bfloat16)
+
+    def put(step, turn):
+        half = (my_half + turn) % halves
+        if (step, turn) == (coarse - 1, 0):
+            return pltpu.make_async_copy(stage.at[half], recv.at[span, :, me], stsem.at[turn])
+        return pltpu.make_async_copy(stage.at[half], send.at[peer(step, turn)], stsem.at[turn])
+
+    load(0, 0).start()
+    for step in range(coarse):
+        if step + 1 < coarse:
+            load(step + 1, (step + 1) % 2).start()
+        channelize(step, step % 2)
+        for turn in range(halves):
+            put(step, turn).start()
+        for turn in range(halves):
+            put(step, turn).wait()
+        for chunk in range(early):
+            for turn in range(halves):
+                if (step, turn) in peers:
+                    outgoing(step, turn, chunk).start()
+    for chunk in range(early, ahead):
+        for step, turn in peers:
+            outgoing(step, turn, chunk).start()
+
+    def fetch(chunk, index, part):
+        return pltpu.make_async_copy(
+            recv.at[part, chunk, :, index], bbuf.at[index, part], bsem.at[index, part]
+        )
+
+    def result(chunk, index):
+        return pltpu.make_async_copy(obuf.at[index], vis.at[chunk * each + index], osem.at[index])
+
+    own_sources = ranks // 2
+    depth = 2 * frames
+
+    def correlate(chunk):
+        backward(chunk).wait_recv()
+        for index in range(each):
+            for part in range(2):
+                fetch(chunk, index, part).start()
+        for index in range(each):
+            for part in range(2):
+                fetch(chunk, index, part).wait()
+
+            @pl.loop(0, own_sources)
+            def _(source):
+                at = pl.multiple_of(source * local_inputs, local_inputs)
+                for part in range(2):
+                    where_real = pl.ds(part * frames, frames)
+                    where_imag = pl.ds(depth + part * frames, frames)
+                    real = bbuf[index, part, span * own_sources + source, 0].T
+                    imag = bbuf[index, part, span * own_sources + source, 1].T
+                    lefts[pl.ds(at, local_inputs), where_real] = real
+                    lefts[pl.ds(at, local_inputs), where_imag] = imag
+                    rights[pl.ds(at, local_inputs), where_real] = imag
+                    rights[pl.ds(at, local_inputs), where_imag] = -real
+
+            @pl.loop(0, ranks // 2)
+            def _(pair):
+                columns = []
+                for side in range(2):
+                    source = pair * 2 + side
+                    columns.append(
+                        jnp.concatenate(
+                            [bbuf[index, part, source, piece] for piece in range(2) for part in range(2)],
+                            axis=0,
+                        )
+                    )
+                block = jnp.concatenate(columns, axis=1)
+                width = 2 * local_inputs
+                real = jnp.dot(lefts[...], block, preferred_element_type=jnp.float32)
+                imag = jnp.dot(rights[...], block, preferred_element_type=jnp.float32)
+                row = span * rows + lax.broadcasted_iota(jnp.int32, (rows, width), 0)
+                column = pair * width + lax.broadcasted_iota(jnp.int32, (rows, width), 1)
+                value = jnp.where(row <= column, real, imag) * scale
+                at = pl.multiple_of(pair * width, width)
+                obuf[index, :, pl.ds(at, width)] = value.astype(jnp.bfloat16)
+
+            result(chunk, index).start()
+        for index in range(each):
+            result(chunk, index).wait()
+
+    @pl.loop(0, chunks)
+    def _(chunk):
+        for step, turn in peers:
+            incoming(step, turn, chunk).wait_recv()
+        forward(chunk).start()
+
+        @pl.when(chunk + ahead < chunks)
+        def _():
+            for step, turn in peers:
+                outgoing(step, turn, chunk + ahead).start()
+
+        @pl.when(chunk > 0)
+        def _():
+            correlate(chunk - 1)
+
+    correlate(chunks - 1)
+
+    @pl.loop(0, chunks)
+    def _(chunk):
+        for step, turn in peers:
+            outgoing(step, turn, chunk).wait_send()
+        forward(chunk).wait_send()
+
+
+def fused(voltages, gains):
+    coarse, local_inputs, samples = voltages.shape[1:]
+    ranks = lax.axis_size("inp")
+    frames = samples // FINE
+    halves = ranks // coarse
+    owned = FINE // halves
+    each = 2
+    chunks = owned // each
+    rows = ranks * local_inputs // 2
+    columns = ranks * local_inputs
+    high, low = filter_rows(FINE, TAPS, 4)
+    gain_rows = jnp.transpose(gains, (1, 0, 3, 2))
+    scale = 1.0 / (2 * frames)
+    dims = (ranks, coarse, chunks, each, local_inputs, frames, scale)
+    bf16 = jnp.bfloat16
+    anywhere = pl.BlockSpec(memory_space=pl.ANY)
+    inside = pl.BlockSpec(memory_space=pltpu.VMEM)
+    flops = 4 * owned * rows * columns * 4 * frames
+    vis, _, _ = pl.pallas_call(
+        functools.partial(fused_kernel, dims),
+        out_shape=(
+            jax.ShapeDtypeStruct((owned, rows, columns), bf16),
+            jax.ShapeDtypeStruct((ranks, chunks, each, 2, frames, local_inputs), bf16),
+            jax.ShapeDtypeStruct((2, chunks, ranks, each, 2, frames, local_inputs), bf16),
+        ),
+        in_specs=[anywhere, inside, inside, inside],
+        out_specs=(anywhere, anywhere, anywhere),
+        scratch_shapes=[
+            pltpu.VMEM((2, 2, local_inputs, samples + TAPS * FINE), bf16),
+            pltpu.VMEM((frames * 2 * FINE, local_inputs), jnp.float32),
+            pltpu.VMEM((halves, chunks, each, 2, frames, local_inputs), bf16),
+            pltpu.VMEM((each, 2, ranks, 2, frames, local_inputs), bf16),
+            pltpu.VMEM((rows, 4 * frames), bf16),
+            pltpu.VMEM((rows, 4 * frames), bf16),
+            pltpu.VMEM((each, rows, columns), bf16),
+            pltpu.SemaphoreType.DMA((2,)),
+            pltpu.SemaphoreType.DMA((halves,)),
+            pltpu.SemaphoreType.DMA((chunks, ranks)),
+            pltpu.SemaphoreType.DMA((chunks, ranks)),
+            pltpu.SemaphoreType.DMA((chunks,)),
+            pltpu.SemaphoreType.DMA((chunks,)),
+            pltpu.SemaphoreType.DMA((each, 2)),
+            pltpu.SemaphoreType.DMA((each,)),
+        ],
+        compiler_params=pltpu.CompilerParams(
+            collective_id=0, has_side_effects=True, vmem_limit_bytes=60 * 1024 * 1024
+        ),
+        cost_estimate=pl.CostEstimate(flops=flops, bytes_accessed=2 * voltages.size * 8, transcendentals=0),
+    )(voltages, gain_rows, jnp.asarray(high), jnp.asarray(low))
+    return vis
+
+
+def chosen(voltages, gains):
+    coarse, local_inputs, samples = voltages.shape[1:]
+    ranks, spans = lax.axis_size("inp"), lax.axis_size("span")
+    fits = (
+        spans == 2
+        and local_inputs % 128 == 0
+        and ranks % coarse == 0
+        and ranks % 2 == 0
+        and FINE % (2 * (ranks // coarse)) == 0
+        and samples % (16 * FINE) == 0
+    )
+    return fused(voltages, gains) if fits else local(voltages, gains)
+
+
 def solution(mesh):
     placed = (P(None, "beam", "inp", "span"), P(None, "beam", "inp", None))
     return jax.shard_map(
-        local,
+        chosen,
         mesh=mesh,
         in_specs=placed,
         out_specs=P(("beam", "inp"), "span", None),

time: 868 us -> 437 us (0.50)
  Pallas kernels: 0 us -> 418 us
  blocking collectives: 366 us -> 0 us
  local copies, waits for them, and re-layouts: 238 us -> 15.5 us
  matrix products: 155 us -> 0 us
  waiting for transfers between devices: 52.3 us -> 0 us
  other arithmetic: 37.4 us -> 0 us
  between operations: 14.2 us -> 0.01 us
    pallas_call x0 -> x1, Pallas kernels: none -> 418 us  [fused(): pl.pallas_call(functools.partial(fused_kernel, dims), out_shape=(jax.Shap...]
    all_to_all x1 -> x0, blocking collectives: 366 us -> none  [local(): lax.all_to_all(outgoing, 'inp', split_axis=1, concat_axis=2, tiled=True)]
    dot_general x4 -> x0, matrix products: 155 us -> none  [the longest x1 44.4 us: local(): jnp.einsum('atcnmp,atpbk->bcknm', stacked, filter_high, preferred_element...]
    another operation x7 -> x0, local copies, waits for them, and re-layouts: 148 us -> none  [the longest x4 123 us: local(): jnp.stack([padded[..., tap_index * FINE:tap_index * FINE + samples] for t...]
    all_gather x1 -> x0, waiting for transfers between devices: 52.3 us -> none  [local(): frame_piece = lax.all_gather(turned, 'span', axis=3, tiled=True)]
    slice x2 -> x0, local copies, waits for them, and re-layouts: 32.5 us -> none  [the longest x1 32.5 us: local(): padded[..., tap_index * FINE:tap_index * FINE + samples]]
    squeeze x2 -> x0, local copies, waits for them, and re-layouts: 29.9 us -> none  [the longest x1 22.5 us: local(): left_all = jnp.concatenate([frame_piece[0], frame_piece[1]], axis=-1)]
    another operation x9 -> x0, other arithmetic: 25.9 us -> none
  transfers between devices with their start and end apart: 1 -> 0, of which waited for: 1 -> 0; matrix products, arithmetic and copies ran while one was open for 0% -> 0% of each run, Pallas kernels for 0% -> 0%
where the time goes in v1:
time: 437 us; the launch traced here: 433 us
  Pallas kernels  418 us (96%)
  local copies, waits for them, and re-layouts  15.5 us (4%)
    pallas_call x1, Pallas kernels, fused(): pl.pallas_call(functools.partial(fused_kernel, dims), out_shape=(jax.Shap...  418 us
    unnamed x2, local copies, waits for them, and re-layouts  15.5 us

profile of v1, /device:TPU:13, one launch (start us, length us, event | category | flops | bytes accessed | tf_op | source)
XLA Modules:
  0.0 433.3 jit_solution(10740629917891601425)
XLA Ops:
  0.0 1.6 copy.7
  1.6 417.8 %shard_map.46 = (bf16[16,512,1024]{2,1,0:T(8,128)(2,1)}, bf16[8,8,2,2,256,128]{5,4,3,2,1,0:T(8,128)(2,1)}, bf16[2,8,8,2,2,256,128]{6,5,4,3,2,1,0:T(8,128)(2,1)}) custom-call(bf16[2,4,128,8192]{3,2,1,0:T(8,128)(2,1)} %volt.1, f32[4,2,32,128]{3,2,1,0:T(8,128)} %bitcast.3, bf16[256,512]{1,0:T(8,128)(2,1)} %constant.4.clone.high, bf16[256,512]{1,0:T(8,128)(2,1)} %constant.5.clone.low), custom_call_target="tpu_custom_call" | custom-call | flops 34359738368 | bytes 134217728 | tf_op jit(solution)/shard_map/pallas_call | solution.py:368
  419.4 13.9 %copy.9 = bf16[16,512,1024]{2,1,0:T(8,128)(2,1)} copy(bf16[16,512,1024]{2,1,0:T(8,128)(2,1)} %get-tuple-element.6) | data formatting | bytes 33554432

commit v2 on v1

--- a/solution.py
+++ b/solution.py
@@ -126,15 +126,15 @@
 
 def fused_kernel(
     dims, volt, gains, high, low, vis, send, recv,
-    xbuf, tbuf, stage, bbuf, lefts, rights, obuf,
+    xbuf, tbuf, stage, bbuf, turned, obuf,
     xsem, stsem, ssem, rsem, psend, precv, bsem, osem,
 ):
     ranks, coarse, chunks, each, local_inputs, frames, scale = dims
     halves = ranks // coarse
     samples = frames * FINE
     rows = ranks * local_inputs // 2
-    ahead = min(4, chunks)
-    early = min(2, chunks)
+    ahead = min(8, chunks)
+    early = min(4, chunks)
     beam = lax.axis_index("beam")
     me = lax.axis_index("inp")
     span = lax.axis_index("span")
@@ -206,10 +206,9 @@
     xbuf[1, :, :, pl.ds(samples, TAPS * FINE)] = tail
 
     def channelize(step, slot):
-        block = order_of(step, mine, coarse)
         load(step, slot).wait()
 
-        @pl.loop(0, frames // 8)
+        @pl.loop(0, frames // 8, unroll=2)
         def _(pair):
             base = pl.multiple_of(pair * (8 * FINE), 4 * FINE)
             pieces = []
@@ -230,11 +229,15 @@
             tbuf[pl.ds(at, 8 * FINE), :] = got[:, :local_inputs]
             tbuf[pl.ds(at + 8 * FINE, 8 * FINE), :] = got[:, local_inputs:]
 
-        @pl.loop(0, FINE)
-        def _(fine):
-            half = fine // (chunks * each)
-            chunk = (fine // each) % chunks
-            index = fine % each
+    def weigh(step, turn):
+        block = order_of(step, mine, coarse)
+        half = (my_half + turn) % halves
+
+        @pl.loop(0, chunks * each, unroll=2)
+        def _(own):
+            chunk = own // each
+            index = own % each
+            fine = half * (chunks * each) + own
             real = tbuf[pl.ds(fine, frames, stride=2 * FINE), :]
             imag = tbuf[pl.ds(FINE + fine, frames, stride=2 * FINE), :]
             gain_real = gains[block, 0, pl.ds(fine, 1), :]
@@ -254,12 +257,11 @@
             load(step + 1, (step + 1) % 2).start()
         channelize(step, step % 2)
         for turn in range(halves):
+            weigh(step, turn)
             put(step, turn).start()
-        for turn in range(halves):
             put(step, turn).wait()
-        for chunk in range(early):
-            for turn in range(halves):
-                if (step, turn) in peers:
+            if (step, turn) in peers:
+                for chunk in range(early):
                     outgoing(step, turn, chunk).start()
     for chunk in range(early, ahead):
         for step, turn in peers:
@@ -276,45 +278,61 @@
     own_sources = ranks // 2
     depth = 2 * frames
 
+    def turn_over(index, part):
+        @pl.loop(0, own_sources)
+        def _(source):
+            at = pl.multiple_of(source * local_inputs, local_inputs)
+            where_real = pl.ds(pl.multiple_of(part * frames, frames), frames)
+            where_imag = pl.ds(pl.multiple_of(depth + part * frames, frames), frames)
+            real = bbuf[index, part, span * own_sources + source, 0].T
+            imag = bbuf[index, part, span * own_sources + source, 1].T
+            turned[0, pl.ds(at, local_inputs), where_real] = real
+            turned[0, pl.ds(at, local_inputs), where_imag] = imag
+            turned[1, pl.ds(at, local_inputs), where_real] = imag
+            turned[1, pl.ds(at, local_inputs), where_imag] = -real
+
+    width = 2 * local_inputs
+
+    def columns_of(index, pair):
+        columns = []
+        for side in range(2):
+            source = pair * 2 + side
+            columns.append(
+                jnp.concatenate(
+                    [bbuf[index, part, source, piece] for piece in range(2) for part in range(2)],
+                    axis=0,
+                )
+            )
+        return jnp.concatenate(columns, axis=1)
+
     def correlate(chunk):
-        backward(chunk).wait_recv()
         for index in range(each):
-            for part in range(2):
-                fetch(chunk, index, part).start()
+            fetch(chunk, index, span).start()
         for index in range(each):
-            for part in range(2):
-                fetch(chunk, index, part).wait()
-
-            @pl.loop(0, own_sources)
-            def _(source):
-                at = pl.multiple_of(source * local_inputs, local_inputs)
-                for part in range(2):
-                    where_real = pl.ds(part * frames, frames)
-                    where_imag = pl.ds(depth + part * frames, frames)
-                    real = bbuf[index, part, span * own_sources + source, 0].T
-                    imag = bbuf[index, part, span * own_sources + source, 1].T
-                    lefts[pl.ds(at, local_inputs), where_real] = real
-                    lefts[pl.ds(at, local_inputs), where_imag] = imag
-                    rights[pl.ds(at, local_inputs), where_real] = imag
-                    rights[pl.ds(at, local_inputs), where_imag] = -real
-
-            @pl.loop(0, ranks // 2)
-            def _(pair):
-                columns = []
-                for side in range(2):
-                    source = pair * 2 + side
-                    columns.append(
-                        jnp.concatenate(
-                            [bbuf[index, part, source, piece] for piece in range(2) for part in range(2)],
-                            axis=0,
-                        )
-                    )
-                block = jnp.concatenate(columns, axis=1)
-                width = 2 * local_inputs
-                real = jnp.dot(lefts[...], block, preferred_element_type=jnp.float32)
-                imag = jnp.dot(rights[...], block, preferred_element_type=jnp.float32)
-                row = span * rows + lax.broadcasted_iota(jnp.int32, (rows, width), 0)
-                column = pair * width + lax.broadcasted_iota(jnp.int32, (rows, width), 1)
+            fetch(chunk, index, span).wait()
+            turn_over(index, span)
+            if index == 0:
+                backward(chunk).wait_recv()
+            fetch(chunk, index, 1 - span).start()
+            fetch(chunk, index, 1 - span).wait()
+            turn_over(index, 1 - span)
+
+            @pl.loop(0, ranks // 4)
+            def _(step):
+                pair = (1 - span) * (ranks // 4) + step
+                block = columns_of(index, pair)
+                value = jnp.dot(turned[span], block, preferred_element_type=jnp.float32) * scale
+                at = pl.multiple_of(pair * width, width)
+                obuf[index, :, pl.ds(at, width)] = value.astype(jnp.bfloat16)
+
+            @pl.loop(0, ranks // 4)
+            def _(step):
+                pair = span * (ranks // 4) + step
+                block = columns_of(index, pair)
+                real = jnp.dot(turned[0], block, preferred_element_type=jnp.float32)
+                imag = jnp.dot(turned[1], block, preferred_element_type=jnp.float32)
+                row = lax.broadcasted_iota(jnp.int32, (rows, width), 0)
+                column = step * width + lax.broadcasted_iota(jnp.int32, (rows, width), 1)
                 value = jnp.where(row <= column, real, imag) * scale
                 at = pl.multiple_of(pair * width, width)
                 obuf[index, :, pl.ds(at, width)] = value.astype(jnp.bfloat16)
@@ -334,11 +352,7 @@
             for step, turn in peers:
                 outgoing(step, turn, chunk + ahead).start()
 
-        @pl.when(chunk > 0)
-        def _():
-            correlate(chunk - 1)
-
-    correlate(chunks - 1)
+        correlate(chunk)
 
     @pl.loop(0, chunks)
     def _(chunk):
@@ -353,7 +367,7 @@
     frames = samples // FINE
     halves = ranks // coarse
     owned = FINE // halves
-    each = 2
+    each = 1
     chunks = owned // each
     rows = ranks * local_inputs // 2
     columns = ranks * local_inputs
@@ -379,8 +393,7 @@
             pltpu.VMEM((frames * 2 * FINE, local_inputs), jnp.float32),
             pltpu.VMEM((halves, chunks, each, 2, frames, local_inputs), bf16),
             pltpu.VMEM((each, 2, ranks, 2, frames, local_inputs), bf16),
-            pltpu.VMEM((rows, 4 * frames), bf16),
-            pltpu.VMEM((rows, 4 * frames), bf16),
+            pltpu.VMEM((2, rows, 4 * frames), bf16),
             pltpu.VMEM((each, rows, columns), bf16),
             pltpu.SemaphoreType.DMA((2,)),
             pltpu.SemaphoreType.DMA((halves,)),
@@ -406,8 +419,8 @@
         spans == 2
         and local_inputs % 128 == 0
         and ranks % coarse == 0
-        and ranks % 2 == 0
-        and FINE % (2 * (ranks // coarse)) == 0
+        and ranks % 4 == 0
+        and FINE % (ranks // coarse) == 0
         and samples % (16 * FINE) == 0
     )
     return fused(voltages, gains) if fits else local(voltages, gains)

time: 437 us -> 414 us (0.947)
  Pallas kernels: 418 us -> 397 us
    pallas_call x1, Pallas kernels: 418 us -> 397 us  [fused(): pl.pallas_call(functools.partial(fused_kernel, dims), out_shape=(jax.Shap...]
where the time goes in v2:
time: 414 us; the launch traced here: 413 us
  Pallas kernels  397 us (96%)
  local copies, waits for them, and re-layouts  15.5 us (4%)
    pallas_call x1, Pallas kernels, fused(): pl.pallas_call(functools.partial(fused_kernel, dims), out_shape=(jax.Shap...  397 us
    unnamed x2, local copies, waits for them, and re-layouts  15.5 us

profile of v2, /device:TPU:13, one launch (start us, length us, event | category | flops | bytes accessed | tf_op | source)
XLA Modules:
  0.0 412.7 jit_solution(3195896093220886297)
XLA Ops:
  0.0 1.6 copy.7
  1.6 397.2 %shard_map.46 = (bf16[16,512,1024]{2,1,0:T(8,128)(2,1)}, bf16[8,16,1,2,256,128]{5,4,3,2,1,0:T(8,128)(2,1)}, bf16[2,16,8,1,2,256,128]{6,5,4,3,2,1,0:T(8,128)(2,1)}) custom-call(bf16[2,4,128,8192]{3,2,1,0:T(8,128)(2,1)} %volt.1, f32[4,2,32,128]{3,2,1,0:T(8,128)} %bitcast.3, bf16[256,512]{1,0:T(8,128)(2,1)} %constant.4.clone.high, ...), custom_call_target="tpu_custom_call" | custom-call | flops 34359738368 | bytes 134217728 | tf_op jit(solution)/shard_map/pallas_call | solution.py:382
  398.8 13.9 %copy.9 = bf16[16,512,1024]{2,1,0:T(8,128)(2,1)} copy(bf16[16,512,1024]{2,1,0:T(8,128)(2,1)} %get-tuple-element.6) | data formatting | bytes 33554432

commit v3 on v2

--- a/solution.py
+++ b/solution.py
@@ -124,6 +124,107 @@
     return high, low
 
 
+def products(dims, span, bbuf, turned, obuf):
+    ranks, _, _, _, local_inputs, frames, scale = dims
+    rows = ranks * local_inputs // 2
+    own_sources = ranks // 2
+    depth = 2 * frames
+
+    def turn_over(index, part):
+        @pl.loop(0, own_sources)
+        def _(source):
+            at = pl.multiple_of(source * local_inputs, local_inputs)
+            where_real = pl.ds(pl.multiple_of(part * frames, frames), frames)
+            where_imag = pl.ds(pl.multiple_of(depth + part * frames, frames), frames)
+            real = bbuf[index, part, span * own_sources + source, 0].T
+            imag = bbuf[index, part, span * own_sources + source, 1].T
+            turned[0, pl.ds(at, local_inputs), where_real] = real
+            turned[0, pl.ds(at, local_inputs), where_imag] = imag
+            turned[1, pl.ds(at, local_inputs), where_real] = imag
+            turned[1, pl.ds(at, local_inputs), where_imag] = -real
+
+    width = 2 * local_inputs
+
+    def columns_of(index, pair):
+        columns = []
+        for side in range(2):
+            source = pair * 2 + side
+            columns.append(
+                jnp.concatenate(
+                    [bbuf[index, part, source, piece] for piece in range(2) for part in range(2)],
+                    axis=0,
+                )
+            )
+        return jnp.concatenate(columns, axis=1)
+
+    def multiply(index):
+        @pl.loop(0, ranks // 4)
+        def _(step):
+            pair = (1 - span) * (ranks // 4) + step
+            block = columns_of(index, pair)
+            value = jnp.dot(turned[span], block, preferred_element_type=jnp.float32) * scale
+            at = pl.multiple_of(pair * width, width)
+            obuf[index, :, pl.ds(at, width)] = value.astype(jnp.bfloat16)
+
+        @pl.loop(0, ranks // 4)
+        def _(step):
+            pair = span * (ranks // 4) + step
+            block = columns_of(index, pair)
+            real = jnp.dot(turned[0], block, preferred_element_type=jnp.float32)
+            imag = jnp.dot(turned[1], block, preferred_element_type=jnp.float32)
+            row = lax.broadcasted_iota(jnp.int32, (rows, width), 0)
+            column = step * width + lax.broadcasted_iota(jnp.int32, (rows, width), 1)
+            value = jnp.where(row <= column, real, imag) * scale
+            at = pl.multiple_of(pair * width, width)
+            obuf[index, :, pl.ds(at, width)] = value.astype(jnp.bfloat16)
+
+    return turn_over, multiply
+
+
+def finish_kernel(dims, part_vis, recv, vis, kept, bbuf, turned, obuf, insem, outsem, bsem, osem):
+    chunks, each = dims[2], dims[3]
+    late = min(2, chunks - 1)
+    first = chunks - late
+    span = lax.axis_index("span")
+    turn_over, multiply = products(dims, span, bbuf, turned, obuf)
+
+    def fetch(slot, part):
+        return pltpu.make_async_copy(
+            recv.at[part, first + slot // each, :, slot % each], bbuf.at[slot, part], bsem.at[slot, part]
+        )
+
+    def take(channel):
+        return pltpu.make_async_copy(part_vis.at[channel], kept.at[channel], insem.at[channel])
+
+    def give(channel):
+        return pltpu.make_async_copy(kept.at[channel], vis.at[channel], outsem.at[channel])
+
+    def result(slot):
+        return pltpu.make_async_copy(obuf.at[slot], vis.at[first * each + slot], osem.at[slot])
+
+    for part in range(2):
+        fetch(0, part).start()
+    for channel in range(first * each):
+        take(channel).start()
+    for slot in range(1, late * each):
+        for part in range(2):
+            fetch(slot, part).start()
+    for slot in range(late * each):
+        for part in range(2):
+            fetch(slot, part).wait()
+            turn_over(slot, part)
+        multiply(slot)
+        result(slot).start()
+        if slot == 0:
+            for channel in range(first * each):
+                take(channel).wait()
+                give(channel).start()
+    for slot in range(late * each):
+        result(slot).wait()
+    for channel in range(first * each):
+        give(channel).wait()
+
+
 def fused_kernel(
     dims, volt, gains, high, low, vis, send, recv,
     xbuf, tbuf, stage, bbuf, turned, obuf,
@@ -135,6 +236,7 @@
     rows = ranks * local_inputs // 2
     ahead = min(8, chunks)
     early = min(4, chunks)
+    late = min(2, chunks - 1)
     beam = lax.axis_index("beam")
     me = lax.axis_index("inp")
     span = lax.axis_index("span")
@@ -275,35 +377,7 @@
     def result(chunk, index):
         return pltpu.make_async_copy(obuf.at[index], vis.at[chunk * each + index], osem.at[index])
 
-    own_sources = ranks // 2
-    depth = 2 * frames
-
-    def turn_over(index, part):
-        @pl.loop(0, own_sources)
-        def _(source):
-            at = pl.multiple_of(source * local_inputs, local_inputs)
-            where_real = pl.ds(pl.multiple_of(part * frames, frames), frames)
-            where_imag = pl.ds(pl.multiple_of(depth + part * frames, frames), frames)
-            real = bbuf[index, part, span * own_sources + source, 0].T
-            imag = bbuf[index, part, span * own_sources + source, 1].T
-            turned[0, pl.ds(at, local_inputs), where_real] = real
-            turned[0, pl.ds(at, local_inputs), where_imag] = imag
-            turned[1, pl.ds(at, local_inputs), where_real] = imag
-            turned[1, pl.ds(at, local_inputs), where_imag] = -real
-
-    width = 2 * local_inputs
-
-    def columns_of(index, pair):
-        columns = []
-        for side in range(2):
-            source = pair * 2 + side
-            columns.append(
-                jnp.concatenate(
-                    [bbuf[index, part, source, piece] for piece in range(2) for part in range(2)],
-                    axis=0,
-                )
-            )
-        return jnp.concatenate(columns, axis=1)
+    turn_over, multiply = products(dims, span, bbuf, turned, obuf)
 
     def correlate(chunk):
         for index in range(each):
@@ -317,26 +391,7 @@
             fetch(chunk, index, 1 - span).wait()
             turn_over(index, 1 - span)
 
-            @pl.loop(0, ranks // 4)
-            def _(step):
-                pair = (1 - span) * (ranks // 4) + step
-                block = columns_of(index, pair)
-                value = jnp.dot(turned[span], block, preferred_element_type=jnp.float32) * scale
-                at = pl.multiple_of(pair * width, width)
-                obuf[index, :, pl.ds(at, width)] = value.astype(jnp.bfloat16)
-
-            @pl.loop(0, ranks // 4)
-            def _(step):
-                pair = span * (ranks // 4) + step
-                block = columns_of(index, pair)
-                real = jnp.dot(turned[0], block, preferred_element_type=jnp.float32)
-                imag = jnp.dot(turned[1], block, preferred_element_type=jnp.float32)
-                row = lax.broadcasted_iota(jnp.int32, (rows, width), 0)
-                column = step * width + lax.broadcasted_iota(jnp.int32, (rows, width), 1)
-                value = jnp.where(row <= column, real, imag) * scale
-                at = pl.multiple_of(pair * width, width)
-                obuf[index, :, pl.ds(at, width)] = value.astype(jnp.bfloat16)
-
+            multiply(index)
             result(chunk, index).start()
         for index in range(each):
             result(chunk, index).wait()
@@ -352,7 +407,13 @@
             for step, turn in peers:
                 outgoing(step, turn, chunk + ahead).start()
 
-        correlate(chunk)
+        @pl.when(chunk < chunks - late)
+        def _():
+            correlate(chunk)
+
+        @pl.when(chunk >= chunks - late)
+        def _():
+            backward(chunk).wait_recv()
 
     @pl.loop(0, chunks)
     def _(chunk):
@@ -379,10 +440,12 @@
     anywhere = pl.BlockSpec(memory_space=pl.ANY)
     inside = pl.BlockSpec(memory_space=pltpu.VMEM)
     flops = 4 * owned * rows * columns * 4 * frames
-    vis, _, _ = pl.pallas_call(
+    late = min(2, chunks - 1)
+    first = (chunks - late) * each
+    part_vis, _, recv = pl.pallas_call(
         functools.partial(fused_kernel, dims),
         out_shape=(
-            jax.ShapeDtypeStruct((owned, rows, columns), bf16),
+            jax.ShapeDtypeStruct((first, rows, columns), bf16),
             jax.ShapeDtypeStruct((ranks, chunks, each, 2, frames, local_inputs), bf16),
             jax.ShapeDtypeStruct((2, chunks, ranks, each, 2, frames, local_inputs), bf16),
         ),
@@ -409,7 +472,24 @@
         ),
         cost_estimate=pl.CostEstimate(flops=flops, bytes_accessed=2 * voltages.size * 8, transcendentals=0),
     )(voltages, gain_rows, jnp.asarray(high), jnp.asarray(low))
-    return vis
+    slots = late * each
+    return pl.pallas_call(
+        functools.partial(finish_kernel, dims),
+        out_shape=jax.ShapeDtypeStruct((owned, rows, columns), bf16),
+        in_specs=[anywhere, anywhere],
+        out_specs=anywhere,
+        scratch_shapes=[
+            pltpu.VMEM((first, rows, columns), bf16),
+            pltpu.VMEM((slots, 2, ranks, 2, frames, local_inputs), bf16),
+            pltpu.VMEM((2, rows, 4 * frames), bf16),
+            pltpu.VMEM((slots, rows, columns), bf16),
+            pltpu.SemaphoreType.DMA((first,)),
+            pltpu.SemaphoreType.DMA((first,)),
+            pltpu.SemaphoreType.DMA((slots, 2)),
+            pltpu.SemaphoreType.DMA((slots,)),
+        ],
+        compiler_params=pltpu.CompilerParams(vmem_limit_bytes=60 * 1024 * 1024),
+    )(part_vis, recv)
 
 
 def chosen(voltages, gains):

time: 414 us -> 409 us (0.988)
  local copies, waits for them, and re-layouts: 15.5 us -> 1.57 us
  Pallas kernels: 397 us -> 406 us
    unnamed x2 -> x1, local copies, waits for them, and re-layouts: 15.5 us -> 1.57 us
    pallas_call x0 -> x1, Pallas kernels: none -> 13.7 us  [fused(): pl.pallas_call(functools.partial(finish_kernel, dims), out_shape=jax.Shap...]
    pallas_call x1, Pallas kernels: 397 us -> 392 us  [fused(): pl.pallas_call(functools.partial(fused_kernel, dims), out_shape=(jax.Shap...]
where the time goes in v3:
time: 409 us; the launch traced here: 408 us
  Pallas kernels  406 us (99%)
    pallas_call x1, Pallas kernels, fused(): pl.pallas_call(functools.partial(fused_kernel, dims), out_shape=(jax.Shap...  392 us
    pallas_call x1, Pallas kernels, fused(): pl.pallas_call(functools.partial(finish_kernel, dims), out_shape=jax.Shap...  13.7 us

profile of v3, /device:TPU:13, one launch (start us, length us, event | category | flops | bytes accessed | tf_op | source)
XLA Modules:
  0.0 407.5 jit_solution(18052653230623739606)
XLA Ops:
  0.0 1.6 copy.7
  1.6 392.2 %shard_map.46 = (bf16[14,512,1024]{2,1,0:T(8,128)(2,1)}, bf16[8,16,1,2,256,128]{5,4,3,2,1,0:T(8,128)(2,1)}, bf16[2,16,8,1,2,256,128]{6,5,4,3,2,1,0:T(8,128)(2,1)}) custom-call(bf16[2,4,128,8192]{3,2,1,0:T(8,128)(2,1)} %volt.1, f32[4,2,32,128]{3,2,1,0:T(8,128)} %bitcast.3, bf16[256,512]{1,0:T(8,128)(2,1)} %constant.4.clone.high, ...), custom_call_target="tpu_custom_call" | custom-call | flops 34359738368 | bytes 134217728 | tf_op jit(solution)/shard_map/pallas_call | solution.py:445
  393.8 13.7 %shard_map.47 = bf16[16,512,1024]{2,1,0:T(8,128)(2,1)} custom-call(bf16[14,512,1024]{2,1,0:T(8,128)(2,1)} %get-tuple-element.7.part_vis, bf16[2,16,8,1,2,256,128]{6,5,4,3,2,1,0:T(8,128)(2,1)} %get-tuple-element.8.recv), custom_call_target="tpu_custom_call" | custom-call | tf_op jit(solution)/shard_map/pallas_call | solution.py:476
